TPU v7x, 32 devices: a whole 2x2x4 slice. The times are simulated.
32 devices in a mesh: pipe: 4 (over z), tensor: 4 (over x, core), dp: 2 (over y).
Axes of the slice: x: 2, y: 2, z: 4, core: 2. Of those that a mesh axis runs over, the one named last changes fastest.
Arguments:
- inputs: bfloat16 [2, 128, 4096], P(None, ('tensor', 'dp')), may hold values from -6 to 6
- weights: bfloat16 [2, 4, 4096, 4096], P(None, 'pipe', None, 'tensor'), may hold values from -0.09375 to 0.09375
- norm_gains: float32 [2, 4, 4096], P(None, 'pipe'), may hold values from 0.1 to 1.9
- cotangent: bfloat16 [2, 128, 4096], P(None, ('tensor', 'dp')), may hold values from -6 to 6
Outputs:
- act_factor: bfloat16 [4096, 2, 4, 4096], P(('tensor', 'dp'), None, 'pipe')
- grad_factor: bfloat16 [4096, 2, 4, 4096], P(('tensor', 'dp'), None, 'pipe')
All inputs are finite; a program needn't handle non-finite values.
Results may differ from a plain program's by a relative error of at most 0.025.
Values may be sent and summed in bfloat16 or wider, within the bound.
A program may use at most 192 MiB of HBM per device.

v0:
```python
import jax
import jax.numpy as jnp
from jax import lax
from jax.sharding import PartitionSpec as P

EPSILON = 1e-05


def passed_along(array, axis, by):
    peers = lax.axis_size(axis)
    return lax.ppermute(array, axis, [(i, (i + by) % peers) for i in range(peers)])


def normalize(hidden, gain_row):
    hidden_wide = hidden.astype(jnp.float32)
    inverse_rms = lax.rsqrt(jnp.mean(hidden_wide * hidden_wide, axis=-1, keepdims=True) + EPSILON)
    normed = (hidden_wide * inverse_rms * gain_row).astype(jnp.bfloat16)
    return (hidden_wide, inverse_rms, normed)


def rounded(values):
    return lax.optimization_barrier(values.astype(jnp.bfloat16)).astype(jnp.float32)


def body(inputs, weights, norm_gains, cotangent):
    micro_count, shard_rows, features = inputs.shape
    slot_count = weights.shape[0]
    quarter = weights.shape[3]
    tensor_count = lax.axis_size("tensor")
    pipe_count = lax.axis_size("pipe")
    dp_count = lax.axis_size("dp")
    layer_count = slot_count * pipe_count
    section_index = lax.axis_index("pipe")
    column = lax.axis_index("tensor")
    tick_count = micro_count + layer_count - 1
    group_rows = tensor_count * shard_rows
    group_size = micro_count * group_rows
    stash_count = slot_count * micro_count + 1
    own_rows = quarter // dp_count
    inv_tokens = 1.0 / (micro_count * group_rows * dp_count)
    row_base = column * quarter
    normed_stash = jnp.zeros((stash_count, group_rows, features), jnp.bfloat16)
    hidden_stash = jnp.zeros((stash_count, shard_rows, features), jnp.bfloat16)
    grad_stash = jnp.zeros((stash_count, group_rows, features), jnp.bfloat16)
    received = jnp.zeros((shard_rows, features), jnp.bfloat16)
    for moment in range(tick_count):
        micro_index = (moment - section_index) % pipe_count
        layer_index = moment - micro_index
        usable = (micro_index < micro_count) & (layer_index >= 0) & (layer_index < layer_count)
        slot_index = jnp.clip(layer_index // pipe_count, 0, slot_count - 1)
        target = jnp.where(usable, slot_index * micro_count + micro_index, stash_count - 1)
        if moment < micro_count:
            current = jnp.where(section_index == 0, inputs[moment], received)
        else:
            current = received
        weight = lax.dynamic_index_in_dim(weights, slot_index, 0, keepdims=False)[0]
        gain_row = lax.dynamic_index_in_dim(norm_gains, slot_index, 0, keepdims=False)[0]
        hidden_wide, inverse_rms, normed = normalize(current, gain_row)
        gathered = lax.all_gather(normed, "tensor", axis=0, tiled=True)
        normed_stash = lax.dynamic_update_index_in_dim(normed_stash, gathered, target, 0)
        hidden_stash = lax.dynamic_update_index_in_dim(hidden_stash, current, target, 0)
        if moment + 1 < tick_count:
            active = usable & (layer_index + 1 < layer_count)
            product = lax.cond(
                active,
                lambda: jnp.dot(gathered, weight, preferred_element_type=jnp.float32).astype(
                    jnp.bfloat16
                ),
                lambda: jnp.zeros((group_rows, quarter), jnp.bfloat16),
            )
            returned = lax.all_to_all(product, "tensor", split_axis=0, concat_axis=1, tiled=True)
            following = (hidden_wide + returned.astype(jnp.float32)).astype(jnp.bfloat16)
            received = passed_along(following, "pipe", 1)
    act_tokens = normed_stash[: stash_count - 1].reshape(slot_count, group_size, features)
    received = jnp.zeros((shard_rows, features), jnp.bfloat16)
    for moment in range(tick_count):
        micro_index = (section_index + 1 - layer_count + moment) % pipe_count
        depth = moment - micro_index
        layer_index = layer_count - 1 - depth
        usable = (micro_index < micro_count) & (depth >= 0) & (depth < layer_count)
        slot_index = jnp.clip(layer_index // pipe_count, 0, slot_count - 1)
        target = jnp.where(usable, slot_index * micro_count + micro_index, stash_count - 1)
        if moment < micro_count:
            current = jnp.where(section_index == pipe_count - 1, cotangent[moment], received)
        else:
            current = received
        gathered = lax.all_gather(current, "tensor", axis=0, tiled=True)
        grad_stash = lax.dynamic_update_index_in_dim(grad_stash, gathered, target, 0)
        if moment + 1 < tick_count:
            active = usable & (layer_index > 0)
            weight = lax.dynamic_index_in_dim(weights, slot_index, 0, keepdims=False)[0]
            gain_row = lax.dynamic_index_in_dim(norm_gains, slot_index, 0, keepdims=False)[0]
            own_columns = lax.dynamic_slice_in_dim(gathered, row_base, quarter, 1)

            def partial_rows(
                row_start, row_total, own_columns=own_columns, weight=weight, active=active
            ):
                piece = own_columns
                return lax.cond(
                    active,
                    lambda: lax.dot_general(
                        piece, weight, (((1,), (1,)), ((), ())), preferred_element_type=jnp.float32
                    ),
                    lambda: jnp.zeros((row_total, features), jnp.float32),
                )

            back_sum = lax.psum_scatter(
                partial_rows(jnp.int32(0), shard_rows * lax.axis_size("tensor")).astype(
                    jnp.bfloat16
                ),
                "tensor",
                scatter_dimension=0,
                tiled=True,
            ).astype(jnp.float32)
            stored = lax.dynamic_index_in_dim(hidden_stash, target, 0, keepdims=False)
            hidden_wide = stored.astype(jnp.float32)
            inverse_rms = lax.rsqrt(
                jnp.mean(hidden_wide * hidden_wide, axis=-1, keepdims=True) + EPSILON
            )
            scaled = gain_row * back_sum
            inner = jnp.mean(hidden_wide * scaled, axis=-1, keepdims=True)
            following = (
                current.astype(jnp.float32)
                + inverse_rms * scaled
                - inverse_rms**3 * hidden_wide * inner
            ).astype(jnp.bfloat16)
            received = passed_along(following, "pipe", -1)
    grad_tokens = grad_stash[: stash_count - 1].reshape(slot_count, group_size, features)
    own_base = (column * dp_count + lax.axis_index("dp")) * own_rows
    empty = jnp.zeros((own_rows, slot_count, 1, features), jnp.float32)
    pieces = (
        lax.all_gather(act_tokens, "dp", axis=1, tiled=True),
        lax.all_gather(grad_tokens, "dp", axis=1, tiled=True),
    )

    def one_group(group_pick, totals):
        updated = []
        for factor_pick in range(2):
            tokens_block = lax.dynamic_slice_in_dim(
                pieces[factor_pick], group_pick * group_size, group_size, 1
            )
            partials = []
            for slot_pick in range(slot_count):
                tokens_one = tokens_block[slot_pick]
                columns = lax.dynamic_slice_in_dim(tokens_one, own_base, own_rows, 1)
                gram = lax.dot_general(
                    columns,
                    tokens_one,
                    (((0,), (0,)), ((), ())),
                    preferred_element_type=jnp.float32,
                )
                partials.append(rounded(gram * inv_tokens))
            updated.append(totals[factor_pick] + jnp.stack(partials, 1)[:, :, None, :])
        return (updated[0], updated[1])

    act_total, grad_total = lax.fori_loop(
        0, pieces[0].shape[1] // group_size, one_group, (empty, empty)
    )
    act_factor = act_total.astype(jnp.bfloat16)
    grad_factor = grad_total.astype(jnp.bfloat16)
    return (act_factor, grad_factor)


def solution(mesh):
    in_specs = (
        P(None, ("tensor", "dp"), None),
        P(None, "pipe", None, "tensor"),
        P(None, "pipe", None),
        P(None, ("tensor", "dp"), None),
    )
    out_specs = (P(("tensor", "dp"), None, "pipe", None), P(("tensor", "dp"), None, "pipe", None))
    return jax.shard_map(body, mesh=mesh, in_specs=in_specs, out_specs=out_specs, check_vma=False)
```

profile of v0, /device:TPU:0, one launch (start us, length us, event | category | flops | bytes accessed | tf_op | source)
XLA Modules:
  0.0 747.0 jit_solution(15114251936575644437)
XLA Ops:
  12.7 8.6 %all_gather.60 = bf16[64,4096]{1,0:T(8,128)(2,1)S(1)} all-gather(bf16[16,4096]{1,0:T(8,128)(2,1)S(1)} %fusion.157), channel_id=1, replica_groups=mesh['pipe'=4,'tensor'=4,'dp'=2] {'tensor'}, dimensions={0}, use_global_device_ids=true | all-gather | bytes 655360 | tf_op jit(solution)/shard_map/all_gather | solution.py:59
  21.4 5.6 conditional.16
  21.4 5.6 fusion.6
  30.4 4.5 all-to-all-done
  35.2 6.6 collective-permute-done
  42.1 7.0 all_gather.61
  49.1 5.1 conditional.17
  49.1 5.1 fusion.16
  54.2 7.0 all_to_all.104
  61.4 6.7 collective-permute-done.1
  68.4 7.0 all_gather.62
  75.4 7.0 all_to_all.105
  82.4 3.6 collective-permute-start.2
  89.5 7.0 all_gather.63
  96.5 7.1 all_to_all.106
  105.5 6.1 collective-permute-done.3
  111.9 7.0 all_gather.64
  118.8 5.8 conditional.20
  118.8 5.8 fusion.46
  128.0 4.5 all-to-all-done.4
  132.7 7.0 all-gather
  141.3 7.7 %all_gather.65 = bf16[64,4096]{1,0:T(8,128)(2,1)} all-gather(bf16[16,4096]{1,0:T(8,128)(2,1)S(1)} %fusion.145), channel_id=1, replica_groups=mesh['pipe'=4,'tensor'=4,'dp'=2] {'tensor'}, dimensions={0}, use_global_device_ids=true | all-gather | bytes 655360 | tf_op jit(solution)/shard_map/all_gather | solution.py:59
  149.0 5.8 conditional.21
  149.0 5.8 fusion.56
  158.2 4.5 all-to-all-done.5
  162.9 7.9 %collective-permute-done.5 = bf16[16,4096]{1,0:T(8,128)(2,1)S(1)} collective-permute-done((bf16[16,4096]{1,0:T(8,128)(2,1)S(1)}, bf16[16,4096]{1,0:T(8,128)(2,1)S(1)}, u32[]{:S(2)}, u32[]{:S(2)}) %collective-permute-start.5) | collective-permute-done | bytes 131104 | tf_op jit(solution)/shard_map/ppermute | solution.py:11
  171.0 7.0 all_gather.66
  182.0 4.5 all-to-all-done.6
  189.1 4.4 collective-permute-done.6
  193.7 7.0 all_gather.67
  204.7 4.5 all-to-all-done.7
  210.8 5.4 collective-permute-done.7
  219.2 6.3 collective-permute-start.8
  228.0 7.0 all_gather.71
  238.5 26.8 %reduce-scatter.11.cloned.1.call-done = bf16[16,4096]{1,0:T(8,128)(2,1)} async-done(((bf16[64,4096]{1,0:T(8,128)(2,1)}), bf16[16,4096]{1,0:T(8,128)(2,1)}) %reduce-scatter.11.cloned.1.call-update) | async-done | bytes 131088 | tf_op jit(solution)/shard_map/reduce_scatter | solution.py:107
  274.4 7.3 all_gather.72
  285.7 23.5 %reduce-scatter.13.cloned.1.call-done = bf16[16,4096]{1,0:T(8,128)(2,1)} async-done(((bf16[64,4096]{1,0:T(8,128)(2,1)}), bf16[16,4096]{1,0:T(8,128)(2,1)}) %reduce-scatter.13.cloned.1.call-update) | async-done | bytes 131088 | tf_op jit(solution)/shard_map/reduce_scatter | solution.py:107
  311.4 3.4 collective-permute-start.10
  317.3 6.9 all_gather.73
  324.3 6.9 conditional.27
  324.3 6.9 fusion.95
  334.4 16.6 %reduce-scatter.15.cloned.1.call-done = bf16[16,4096]{1,0:T(8,128)(2,1)} async-done(((bf16[64,4096]{1,0:T(8,128)(2,1)}), bf16[16,4096]{1,0:T(8,128)(2,1)}) %reduce-scatter.15.cloned.1.call-update) | async-done | bytes 131088 | tf_op jit(solution)/shard_map/reduce_scatter | solution.py:107
  359.1 6.9 all_gather.74
  366.0 6.9 conditional.28
  366.0 6.9 fusion.100
  376.1 20.3 %reduce-scatter.17.cloned.1.call-done = bf16[16,4096]{1,0:T(8,128)(2,1)} async-done(((bf16[64,4096]{1,0:T(8,128)(2,1)}), bf16[16,4096]{1,0:T(8,128)(2,1)}) %reduce-scatter.17.cloned.1.call-update) | async-done | bytes 131088 | tf_op jit(solution)/shard_map/reduce_scatter | solution.py:107
  404.5 6.9 all_gather.75
  415.5 26.3 %reduce-scatter.19.cloned.1.call-done = bf16[16,4096]{1,0:T(8,128)(2,1)} async-done(((bf16[64,4096]{1,0:T(8,128)(2,1)}), bf16[16,4096]{1,0:T(8,128)(2,1)}) %reduce-scatter.19.cloned.1.call-update) | async-done | bytes 131088 | tf_op jit(solution)/shard_map/reduce_scatter | solution.py:107
  443.9 3.4 collective-permute-start.13
  450.5 6.9 all_gather.76
  459.3 25.9 %reduce-scatter.21.cloned.1.call-done = bf16[16,4096]{1,0:T(8,128)(2,1)} async-done(((bf16[64,4096]{1,0:T(8,128)(2,1)}), bf16[16,4096]{1,0:T(8,128)(2,1)}) %reduce-scatter.21.cloned.1.call-update) | async-done | bytes 131088 | tf_op jit(solution)/shard_map/reduce_scatter | solution.py:107
  490.8 6.9 all_gather.68
  497.8 7.7 %all_gather.77 = bf16[64,4096]{1,0:T(8,128)(2,1)} all-gather(bf16[16,4096]{1,0:T(8,128)(2,1)S(1)} %collective-permute-done.14), channel_id=1, replica_groups=mesh['pipe'=4,'tensor'=4,'dp'=2] {'tensor'}, dimensions={0}, use_global_device_ids=true | all-gather | bytes 655360 | tf_op jit(solution)/shard_map/all_gather | solution.py:87
  519.3 11.0 %reduce-scatter.23.cloned.1.call-done = bf16[16,4096]{1,0:T(8,128)(2,1)} async-done(((bf16[64,4096]{1,0:T(8,128)(2,1)}), bf16[16,4096]{1,0:T(8,128)(2,1)}) %reduce-scatter.23.cloned.1.call-update) | async-done | bytes 131088 | tf_op jit(solution)/shard_map/reduce_scatter | solution.py:107
  538.4 6.5 all_gather.78
  546.4 25.0 %all-gather.4.cloned.1.call-done = bf16[2,256,4096]{2,1,0:T(8,128)(2,1)} async-done(((bf16[2,128,4096]{2,1,0:T(8,128)(2,1)}), bf16[2,256,4096]{2,1,0:T(8,128)(2,1)}) %all-gather.4.cloned.1.call-update) | async-done | bytes 4194320 | tf_op jit(solution)/shard_map/all_gather | solution.py:132
  571.5 58.6 %all-gather.6.cloned.1.call-done = bf16[2,256,4096]{2,1,0:T(8,128)(2,1)} async-done(((bf16[2,128,4096]{2,1,0:T(8,128)(2,1)}), bf16[2,256,4096]{2,1,0:T(8,128)(2,1)}) %all-gather.6.cloned.1.call-update) | async-done | bytes 4194320 | tf_op jit(solution)/shard_map/all_gather | solution.py:133
  630.1 62.1 %while.18 = (s32[]{:T(128)}, f32[512,2,1,4096]{3,0,1,2:T(8,128)}, f32[512,2,1,4096]{3,0,1,2:T(8,128)}, bf16[2,256,4096]{2,1,0:T(8,128)(2,1)}, s32[]{:T(128)}, /*...) while((s32[]{:T(128)}, f32[512,2,1,4096]{3,0,1,2:T(8,128)}, ...), condition=%wide.region_66.67_spmd.clone, body=%wide.region_65.66_spmd.clone.sunk | while | flops 2197815296 | bytes 105390264 | solution.py:156
  632.7 4.6 multiply_convert_fusion.10
  642.5 14.2 %convert_add_fusion.12 = (f32[512,2,1,4096]{3,0,1,2:T(8,128)}, f32[512,2,1,4096]{3,0,1,2:T(8,128)}) fusion(f32[512,2,1,4096]{3,0,1,2:T(8,128)} %get-tuple-element.770, bf16[512,1,4096]{2,0,1:T(8,128)(2,1)S(1)} %bitcast.333, bf16[512,1,4096]{2,0,1:T(8,128)(2,1)S(1)} %bitcast.331, pred[]{:T(512)S(6)} %compare.57, bf16[512,1,4096]{2,0,1:T(8,128)(2,1)} %bitcast.334, ...), kind=kLoop, calls=%fused_computation.88.clone.1 | loop fusion | flops 33554432 | bytes 83886080 | tf_op jit(solution)/shard_map/while/body/eval_jaxpr/add | solution.py:153
  659.2 4.6 multiply_convert_fusion.10
  669.1 23.1 %convert_add_fusion.12 = (f32[512,2,1,4096]{3,0,1,2:T(8,128)}, f32[512,2,1,4096]{3,0,1,2:T(8,128)}) fusion(f32[512,2,1,4096]{3,0,1,2:T(8,128)} %get-tuple-element.770, bf16[512,1,4096]{2,0,1:T(8,128)(2,1)S(1)} %bitcast.333, bf16[512,1,4096]{2,0,1:T(8,128)(2,1)S(1)} %bitcast.331, pred[]{:T(512)S(6)} %compare.57, bf16[512,1,4096]{2,0,1:T(8,128)(2,1)} %bitcast.334, ...), kind=kLoop, calls=%fused_computation.88.clone.1 | loop fusion | flops 33554432 | bytes 83886080 | tf_op jit(solution)/shard_map/while/body/eval_jaxpr/add | solution.py:153
  692.2 28.6 %copy.38 = bf16[512,2,1,4096]{3,1,2,0:T(2,128)(2,1)} copy(f32[512,2,1,4096]{3,0,1,2:T(8,128)} %get-tuple-element.635) | data formatting | bytes 25165824 | tf_op jit(solution)/shard_map/while | solution.py:156
  720.7 18.6 %copy.39 = bf16[512,2,1,4096]{3,1,2,0:T(2,128)(2,1)} copy(f32[512,2,1,4096]{3,0,1,2:T(8,128)S(1)} %copy-done) | data formatting | bytes 25165824 | tf_op jit(solution)/shard_map/while | solution.py:156
  (205 shorter events, 144.5 us)
Async XLA Ops:
  8.0 27.0 %copy-start.3 = (bf16[2,16,4096]{2,1,0:T(8,128)(2,1)S(1)}, bf16[2,16,4096]{2,1,0:T(8,128)(2,1)}, u32[]{:S(2)}) copy-start(bf16[2,16,4096]{2,1,0:T(8,128)(2,1)} %param.38) | copy-start | bytes 786436
  27.0 7.9 %all-to-all-start = ((bf16[4,16,1024]{2,1,0:T(8,128)(2,1)}), bf16[4,16,1024]{2,1,0:T(8,128)(2,1)S(1)}, u32[]{:S(2)}, u32[]{:S(2)}) async-start(bf16[4,16,1024]{2,1,0:T(8,128)(2,1)} %bitcast.29), calls=%async_computation | async-start | bytes 262144 | tf_op jit(solution)/shard_map/all_to_all | solution.py:71
  35.0 6.8 collective-permute-start
  61.3 6.8 collective-permute-start.1
  82.4 6.8 collective-permute-start.2
  96.5 31.5 %copy-start.4 = (bf16[2,16,4096]{2,1,0:T(8,128)(2,1)S(1)}, bf16[2,16,4096]{2,1,0:T(8,128)(2,1)}, u32[]{:S(2)}) copy-start(bf16[2,16,4096]{2,1,0:T(8,128)(2,1)} %param.41) | copy-start | bytes 786436
  103.7 7.9 %collective-permute-start.3 = (bf16[16,4096]{1,0:T(8,128)(2,1)S(1)}, bf16[16,4096]{1,0:T(8,128)(2,1)S(1)}, u32[]{:S(2)}, u32[]{:S(2)}) collective-permute-start(bf16[16,4096]{1,0:T(8,128)(2,1)S(1)} %fusion.138), channel_id=1, source_target_pairs={{0,8},{8,16},{16,24},{24,0},{1,9},{9,17},{17,25},{25,1},{2,10},{10... | collective-permute-start | bytes 393224 | tf_op jit(solution)/shard_map/ppermute | solution.py:11
  124.6 7.9 %all-to-all-start.4 = ((bf16[4,16,1024]{2,1,0:T(8,128)(2,1)}), bf16[4,16,1024]{2,1,0:T(8,128)(2,1)S(1)}, u32[]{:S(2)}, u32[]{:S(2)}) async-start(bf16[4,16,1024]{2,1,0:T(8,128)(2,1)} %bitcast.45), calls=%async_computation.4 | async-start | bytes 262144 | tf_op jit(solution)/shard_map/all_to_all | solution.py:71
  127.9 88.2 %reduce-scatter.9.cloned.1.call-start = ((), (), s32[]{:S(2)}) async-start(), calls=%async_computation.17 | async-start | bytes 655360 | tf_op jit(solution)/shard_map/reduce_scatter | solution.py:107
  132.6 8.4 %collective-permute-start.4 = (bf16[16,4096]{1,0:T(8,128)(2,1)S(1)}, bf16[16,4096]{1,0:T(8,128)(2,1)S(1)}, u32[]{:S(2)}, u32[]{:S(2)}) collective-permute-start(bf16[16,4096]{1,0:T(8,128)(2,1)S(1)} %fusion.142), channel_id=1, source_target_pairs={{0,8},{8,16},{16,24},{24,0},{1,9},{9,17},{17,25},{25,1},{2,10},{10... | collective-permute-start | bytes 393224 | tf_op jit(solution)/shard_map/ppermute | solution.py:11
  139.8 0.8 copy-start.1
  154.8 7.9 %all-to-all-start.5 = ((bf16[4,16,1024]{2,1,0:T(8,128)(2,1)}), bf16[4,16,1024]{2,1,0:T(8,128)(2,1)S(1)}, u32[]{:S(2)}, u32[]{:S(2)}) async-start(bf16[4,16,1024]{2,1,0:T(8,128)(2,1)} %bitcast.49), calls=%async_computation.5 | async-start | bytes 262144 | tf_op jit(solution)/shard_map/all_to_all | solution.py:71
  162.8 7.9 %collective-permute-start.5 = (bf16[16,4096]{1,0:T(8,128)(2,1)S(1)}, bf16[16,4096]{1,0:T(8,128)(2,1)S(1)}, u32[]{:S(2)}, u32[]{:S(2)}) collective-permute-start(bf16[16,4096]{1,0:T(8,128)(2,1)S(1)} %fusion.146), channel_id=1, source_target_pairs={{0,8},{8,16},{16,24},{24,0},{1,9},{9,17},{17,25},{25,1},{2,10},{10... | collective-permute-start | bytes 393224 | tf_op jit(solution)/shard_map/ppermute | solution.py:11
  178.6 7.9 %all-to-all-start.6 = ((bf16[4,16,1024]{2,1,0:T(8,128)(2,1)}), bf16[4,16,1024]{2,1,0:T(8,128)(2,1)S(1)}, u32[]{:S(2)}, u32[]{:S(2)}) async-start(bf16[4,16,1024]{2,1,0:T(8,128)(2,1)} %bitcast.53), calls=%async_computation.6 | async-start | bytes 262144 | tf_op jit(solution)/shard_map/all_to_all | solution.py:71
  186.6 6.8 collective-permute-start.6
  201.3 7.9 %all-to-all-start.7 = ((bf16[4,16,1024]{2,1,0:T(8,128)(2,1)}), bf16[4,16,1024]{2,1,0:T(8,128)(2,1)S(1)}, u32[]{:S(2)}, u32[]{:S(2)}) async-start(bf16[4,16,1024]{2,1,0:T(8,128)(2,1)} %bitcast.57), calls=%async_computation.7 | async-start | bytes 262144 | tf_op jit(solution)/shard_map/all_to_all | solution.py:71
  204.7 60.7 %reduce-scatter.11.cloned.1.call-start = ((), (), s32[]{:S(2)}) async-start(), calls=%async_computation.18 | async-start | bytes 655360 | tf_op jit(solution)/shard_map/reduce_scatter | solution.py:107
  209.3 6.8 collective-permute-start.7
  219.2 8.8 %collective-permute-start.8 = (bf16[16,4096]{1,0:T(8,128)(2,1)S(1)}, bf16[16,4096]{1,0:T(8,128)(2,1)S(1)}, u32[]{:S(2)}, u32[]{:S(2)}) collective-permute-start(bf16[16,4096]{1,0:T(8,128)(2,1)S(1)} %fusion.162), channel_id=1, source_target_pairs={{0,24},{8,0},{16,8},{24,16},{1,25},{9,1},{17,9},{25,17},{2,26},{10... | collective-permute-start | bytes 393224 | tf_op jit(solution)/shard_map/ppermute | solution.py:11
  235.0 0.8 copy-start.2
  235.9 73.4 %reduce-scatter.13.cloned.1.call-start = ((), (), s32[]{:S(2)}) async-start(), calls=%async_computation.19 | async-start | bytes 655360 | tf_op jit(solution)/shard_map/reduce_scatter | solution.py:107
  268.1 6.3 collective-permute-start.9
  282.6 68.5 %reduce-scatter.15.cloned.1.call-start = ((), (), s32[]{:S(2)}) async-start(), calls=%async_computation.20 | async-start | bytes 655360 | tf_op jit(solution)/shard_map/reduce_scatter | solution.py:107
  311.4 6.0 collective-permute-start.10
  331.2 65.1 %reduce-scatter.17.cloned.1.call-start = ((), (), s32[]{:S(2)}) async-start(), calls=%async_computation.21 | async-start | bytes 655360 | tf_op jit(solution)/shard_map/reduce_scatter | solution.py:107
  353.1 6.0 collective-permute-start.11
  373.0 68.7 %reduce-scatter.19.cloned.1.call-start = ((), (), s32[]{:S(2)}) async-start(), calls=%async_computation.22 | async-start | bytes 655360 | tf_op jit(solution)/shard_map/reduce_scatter | solution.py:107
  398.5 6.0 collective-permute-start.12
  412.3 73.0 %reduce-scatter.21.cloned.1.call-start = ((), (), s32[]{:S(2)}) async-start(), calls=%async_computation.23 | async-start | bytes 655360 | tf_op jit(solution)/shard_map/reduce_scatter | solution.py:107
  443.9 6.0 collective-permute-start.13
  449.9 0.6 copy-start.5
  458.5 71.8 %reduce-scatter.23.cloned.1.call-start = ((), (), s32[]{:S(2)}) async-start(), calls=%async_computation.24 | async-start | bytes 655360 | tf_op jit(solution)/shard_map/reduce_scatter | solution.py:107
  487.5 10.3 %collective-permute-start.14 = (bf16[16,4096]{1,0:T(8,128)(2,1)S(1)}, bf16[16,4096]{1,0:T(8,128)(2,1)S(1)}, u32[]{:S(2)}, u32[]{:S(2)}) collective-permute-start(bf16[16,4096]{1,0:T(8,128)(2,1)S(1)} %fusion.192), channel_id=1, source_target_pairs={{0,24},{8,0},{16,8},{24,16},{1,25},{9,1},{17,9},{25,17},{2,26},{10... | collective-permute-start | bytes 393224 | tf_op jit(solution)/shard_map/ppermute | solution.py:11
  506.4 65.1 %all-gather.4.cloned.1.call-start = ((), (), s32[]{:S(2)}) async-start(), calls=%async_computation.16 | async-start | bytes 6291456 | tf_op jit(solution)/shard_map/all_gather | solution.py:132
  512.7 117.4 %all-gather.6.cloned.1.call-start = ((), (), s32[]{:S(2)}) async-start(), calls=%async_computation.25 | async-start | bytes 6291456 | tf_op jit(solution)/shard_map/all_gather | solution.py:133
  532.4 6.0 collective-permute-start.15
  692.2 28.6 %copy-start = (f32[512,2,1,4096]{3,0,1,2:T(8,128)S(1)}, f32[512,2,1,4096]{3,0,1,2:T(8,128)}, u32[]{:S(2)}) copy-start(f32[512,2,1,4096]{3,0,1,2:T(8,128)} %get-tuple-element.634) | copy-start | bytes 50331652
Sparse Core Ops, SparseCore 0:
  140.8 28.8 reduce-scatter.8
  236.0 29.3 reduce-scatter.10
  282.7 26.5 reduce-scatter.12
  331.4 19.5 reduce-scatter.14
  373.1 23.2 reduce-scatter.16
  412.4 29.3 reduce-scatter.18
  458.6 26.6 reduce-scatter.20
  506.5 23.7 reduce-scatter.22
Sparse Core Ops, SparseCore 1:
  512.7 58.7 all-gather.3
  573.5 56.6 all-gather.5
where the time goes:
time: 757 us; the launch traced here: 747 us
  waiting for transfers between devices  306 us (40%)
  blocking collectives  149 us (20%)
  local copies, waits for them, and re-layouts  87.8 us (12%)
  other arithmetic  68.5 us (9%)
  matrix products  61 us (8%)
  starting transfers between devices  56.4 us (7%)
  between operations  17.6 us (2%)
    reduce_scatter x8, waiting for transfers between devices, body(): lax.psum_scatter(partial_rows(jnp.int32(0), shard_rows * lax.axis_size('t...  151 us
    all_gather x9, blocking collectives, body(): gathered = lax.all_gather(normed, 'tensor', axis=0, tiled=True)  65 us
    all_gather x9, blocking collectives, body(): gathered = lax.all_gather(current, 'tensor', axis=0, tiled=True)  63.2 us
    all_gather x1, waiting for transfers between devices, body(): lax.all_gather(grad_tokens, 'dp', axis=1, tiled=True)  58.6 us
    ppermute x16, waiting for transfers between devices, passed_along(): lax.ppermute(array, axis, [(i, (i + by) % peers) for i in range(peers)])  49.2 us
    while x2, local copies, waits for them, and re-layouts, body(): lax.fori_loop(0, pieces[0].shape[1] // group_size, one_group, (empty, emp...  47.2 us
    ppermute x16, starting transfers between devices, passed_along(): lax.ppermute(array, axis, [(i, (i + by) % peers) for i in range(peers)])  39.4 us
    add x2, other arithmetic, one_group(): updated.append(totals[factor_pick] + jnp.stack(partials, 1)[:, :, None, :])  37.3 us
  transfers between devices with their start and end apart: 31, of which 28 were waited for; matrix products, arithmetic and copies ran while one was open for 7% of the time, Pallas kernels for 0%

commit v1 on v0

--- a/solution.py
+++ b/solution.py
@@ -130,7 +130,7 @@
     empty = jnp.zeros((own_rows, slot_count, 1, features), jnp.float32)
     pieces = (
         lax.all_gather(act_tokens, "dp", axis=1, tiled=True),
-        lax.all_gather(grad_tokens, "dp", axis=1, tiled=True),
+        jnp.concatenate(lax.all_gather(grad_tokens, "dp"), axis=1),
     )
 
     def one_group(group_pick, totals):

time: 757 us -> 757 us (level)
  no operation moved by 1% of the time
where the time goes in v1:
time: 757 us; the launch traced here: 747 us
  waiting for transfers between devices  306 us (40%)
  blocking collectives  149 us (20%)
  local copies, waits for them, and re-layouts  87.8 us (12%)
  other arithmetic  68.5 us (9%)
  matrix products  61 us (8%)
  starting transfers between devices  56.4 us (7%)
  between operations  17.6 us (2%)
    reduce_scatter x8, waiting for transfers between devices, body(): lax.psum_scatter(partial_rows(jnp.int32(0), shard_rows * lax.axis_size('t...  151 us
    all_gather x9, blocking collectives, body(): gathered = lax.all_gather(normed, 'tensor', axis=0, tiled=True)  65 us
    all_gather x9, blocking collectives, body(): gathered = lax.all_gather(current, 'tensor', axis=0, tiled=True)  63.2 us
    all_gather x1, waiting for transfers between devices, body(): lax.all_gather(grad_tokens, 'dp')  58.6 us
    ppermute x16, waiting for transfers between devices, passed_along(): lax.ppermute(array, axis, [(i, (i + by) % peers) for i in range(peers)])  49.2 us
    while x2, local copies, waits for them, and re-layouts, body(): lax.fori_loop(0, pieces[0].shape[1] // group_size, one_group, (empty, emp...  47.2 us
    ppermute x16, starting transfers between devices, passed_along(): lax.ppermute(array, axis, [(i, (i + by) % peers) for i in range(peers)])  39.4 us
    add x2, other arithmetic, one_group(): updated.append(totals[factor_pick] + jnp.stack(partials, 1)[:, :, None, :])  37.3 us
  transfers between devices with their start and end apart: 31, of which 28 were waited for; matrix products, arithmetic and copies ran while one was open for 7% of the time, Pallas kernels for 0%

profile of v1, /device:TPU:0, one launch (start us, length us, event | category | flops | bytes accessed | tf_op | source)
XLA Modules:
  0.0 747.0 jit_solution(4871965243520608933)
XLA Ops:
  12.7 8.6 %all_gather.60 = bf16[64,4096]{1,0:T(8,128)(2,1)S(1)} all-gather(bf16[16,4096]{1,0:T(8,128)(2,1)S(1)} %fusion.157), channel_id=1, replica_groups=mesh['pipe'=4,'tensor'=4,'dp'=2] {'tensor'}, dimensions={0}, use_global_device_ids=true | all-gather | bytes 655360 | tf_op jit(solution)/shard_map/all_gather | solution.py:59
  21.4 5.6 conditional.16
  21.4 5.6 fusion.6
  30.4 4.5 all-to-all-done
  35.2 6.6 collective-permute-done
  42.1 7.0 all_gather.61
  49.1 5.1 conditional.17
  49.1 5.1 fusion.16
  54.2 7.0 all_to_all.104
  61.4 6.7 collective-permute-done.1
  68.4 7.0 all_gather.62
  75.4 7.0 all_to_all.105
  82.4 3.6 collective-permute-start.2
  89.5 7.0 all_gather.63
  96.5 7.1 all_to_all.106
  105.5 6.1 collective-permute-done.3
  111.9 7.0 all_gather.64
  118.8 5.8 conditional.20
  118.8 5.8 fusion.46
  128.0 4.5 all-to-all-done.4
  132.7 7.0 all-gather
  141.3 7.7 %all_gather.65 = bf16[64,4096]{1,0:T(8,128)(2,1)} all-gather(bf16[16,4096]{1,0:T(8,128)(2,1)S(1)} %fusion.145), channel_id=1, replica_groups=mesh['pipe'=4,'tensor'=4,'dp'=2] {'tensor'}, dimensions={0}, use_global_device_ids=true | all-gather | bytes 655360 | tf_op jit(solution)/shard_map/all_gather | solution.py:59
  149.0 5.8 conditional.21
  149.0 5.8 fusion.56
  158.2 4.5 all-to-all-done.5
  162.9 7.9 %collective-permute-done.5 = bf16[16,4096]{1,0:T(8,128)(2,1)S(1)} collective-permute-done((bf16[16,4096]{1,0:T(8,128)(2,1)S(1)}, bf16[16,4096]{1,0:T(8,128)(2,1)S(1)}, u32[]{:S(2)}, u32[]{:S(2)}) %collective-permute-start.5) | collective-permute-done | bytes 131104 | tf_op jit(solution)/shard_map/ppermute | solution.py:11
  171.0 7.0 all_gather.66
  182.0 4.5 all-to-all-done.6
  189.1 4.4 collective-permute-done.6
  193.7 7.0 all_gather.67
  204.7 4.5 all-to-all-done.7
  210.8 5.4 collective-permute-done.7
  219.2 6.3 collective-permute-start.8
  228.0 7.0 all_gather.71
  238.5 26.8 %reduce-scatter.11.cloned.1.call-done = bf16[16,4096]{1,0:T(8,128)(2,1)} async-done(((bf16[64,4096]{1,0:T(8,128)(2,1)}), bf16[16,4096]{1,0:T(8,128)(2,1)}) %reduce-scatter.11.cloned.1.call-update) | async-done | bytes 131088 | tf_op jit(solution)/shard_map/reduce_scatter | solution.py:107
  274.4 7.3 all_gather.72
  285.7 23.5 %reduce-scatter.13.cloned.1.call-done = bf16[16,4096]{1,0:T(8,128)(2,1)} async-done(((bf16[64,4096]{1,0:T(8,128)(2,1)}), bf16[16,4096]{1,0:T(8,128)(2,1)}) %reduce-scatter.13.cloned.1.call-update) | async-done | bytes 131088 | tf_op jit(solution)/shard_map/reduce_scatter | solution.py:107
  311.4 3.4 collective-permute-start.10
  317.3 6.9 all_gather.73
  324.3 6.9 conditional.27
  324.3 6.9 fusion.95
  334.4 16.6 %reduce-scatter.15.cloned.1.call-done = bf16[16,4096]{1,0:T(8,128)(2,1)} async-done(((bf16[64,4096]{1,0:T(8,128)(2,1)}), bf16[16,4096]{1,0:T(8,128)(2,1)}) %reduce-scatter.15.cloned.1.call-update) | async-done | bytes 131088 | tf_op jit(solution)/shard_map/reduce_scatter | solution.py:107
  359.1 6.9 all_gather.74
  366.0 6.9 conditional.28
  366.0 6.9 fusion.100
  376.1 20.3 %reduce-scatter.17.cloned.1.call-done = bf16[16,4096]{1,0:T(8,128)(2,1)} async-done(((bf16[64,4096]{1,0:T(8,128)(2,1)}), bf16[16,4096]{1,0:T(8,128)(2,1)}) %reduce-scatter.17.cloned.1.call-update) | async-done | bytes 131088 | tf_op jit(solution)/shard_map/reduce_scatter | solution.py:107
  404.5 6.9 all_gather.75
  415.5 26.3 %reduce-scatter.19.cloned.1.call-done = bf16[16,4096]{1,0:T(8,128)(2,1)} async-done(((bf16[64,4096]{1,0:T(8,128)(2,1)}), bf16[16,4096]{1,0:T(8,128)(2,1)}) %reduce-scatter.19.cloned.1.call-update) | async-done | bytes 131088 | tf_op jit(solution)/shard_map/reduce_scatter | solution.py:107
  443.9 3.4 collective-permute-start.13
  450.5 6.9 all_gather.76
  459.3 25.9 %reduce-scatter.21.cloned.1.call-done = bf16[16,4096]{1,0:T(8,128)(2,1)} async-done(((bf16[64,4096]{1,0:T(8,128)(2,1)}), bf16[16,4096]{1,0:T(8,128)(2,1)}) %reduce-scatter.21.cloned.1.call-update) | async-done | bytes 131088 | tf_op jit(solution)/shard_map/reduce_scatter | solution.py:107
  490.8 6.9 all_gather.68
  497.8 7.7 %all_gather.77 = bf16[64,4096]{1,0:T(8,128)(2,1)} all-gather(bf16[16,4096]{1,0:T(8,128)(2,1)S(1)} %collective-permute-done.14), channel_id=1, replica_groups=mesh['pipe'=4,'tensor'=4,'dp'=2] {'tensor'}, dimensions={0}, use_global_device_ids=true | all-gather | bytes 655360 | tf_op jit(solution)/shard_map/all_gather | solution.py:87
  519.3 11.0 %reduce-scatter.23.cloned.1.call-done = bf16[16,4096]{1,0:T(8,128)(2,1)} async-done(((bf16[64,4096]{1,0:T(8,128)(2,1)}), bf16[16,4096]{1,0:T(8,128)(2,1)}) %reduce-scatter.23.cloned.1.call-update) | async-done | bytes 131088 | tf_op jit(solution)/shard_map/reduce_scatter | solution.py:107
  538.4 6.5 all_gather.78
  546.4 25.0 %all-gather.4.cloned.1.call-done = bf16[2,256,4096]{2,1,0:T(8,128)(2,1)} async-done(((bf16[2,128,4096]{2,1,0:T(8,128)(2,1)}), bf16[2,256,4096]{2,1,0:T(8,128)(2,1)}) %all-gather.4.cloned.1.call-update) | async-done | bytes 4194320 | tf_op jit(solution)/shard_map/all_gather | solution.py:132
  571.5 58.6 %all-gather.6.cloned.1.call-done = bf16[2,2,128,4096]{3,2,0,1:T(8,128)(2,1)} async-done(((bf16[1,2,128,4096]{3,2,0,1:T(8,128)(2,1)}), bf16[2,2,128,4096]{3,2,0,1:T(8,128)(2,1)}) %all-gather.6.cloned.1.call-update) | async-done | bytes 4194320 | tf_op jit(solution)/shard_map/all_gather | solution.py:133
  630.1 62.1 %while.18 = (s32[]{:T(128)}, f32[512,2,1,4096]{3,0,1,2:T(8,128)}, f32[512,2,1,4096]{3,0,1,2:T(8,128)}, bf16[2,256,4096]{2,1,0:T(8,128)(2,1)}, s32[]{:T(128)}, /*...) while((s32[]{:T(128)}, f32[512,2,1,4096]{3,0,1,2:T(8,128)}, ...), condition=%wide.region_66.67_spmd.clone, body=%wide.region_65.66_spmd.clone.sunk | while | flops 2197815296 | bytes 105390264 | solution.py:156
  632.7 4.6 multiply_convert_fusion.10
  642.5 14.2 %convert_add_fusion.12 = (f32[512,2,1,4096]{3,0,1,2:T(8,128)}, f32[512,2,1,4096]{3,0,1,2:T(8,128)}) fusion(f32[512,2,1,4096]{3,0,1,2:T(8,128)} %get-tuple-element.770, bf16[512,1,4096]{2,0,1:T(8,128)(2,1)S(1)} %bitcast.338, bf16[512,1,4096]{2,0,1:T(8,128)(2,1)S(1)} %bitcast.336, pred[]{:T(512)S(6)} %compare.57, bf16[512,1,4096]{2,0,1:T(8,128)(2,1)} %bitcast.339, ...), kind=kLoop, calls=%fused_computation.88.clone.1 | loop fusion | flops 33554432 | bytes 83886080 | tf_op jit(solution)/shard_map/while/body/eval_jaxpr/add | solution.py:153
  659.2 4.6 multiply_convert_fusion.10
  669.1 23.1 %convert_add_fusion.12 = (f32[512,2,1,4096]{3,0,1,2:T(8,128)}, f32[512,2,1,4096]{3,0,1,2:T(8,128)}) fusion(f32[512,2,1,4096]{3,0,1,2:T(8,128)} %get-tuple-element.770, bf16[512,1,4096]{2,0,1:T(8,128)(2,1)S(1)} %bitcast.338, bf16[512,1,4096]{2,0,1:T(8,128)(2,1)S(1)} %bitcast.336, pred[]{:T(512)S(6)} %compare.57, bf16[512,1,4096]{2,0,1:T(8,128)(2,1)} %bitcast.339, ...), kind=kLoop, calls=%fused_computation.88.clone.1 | loop fusion | flops 33554432 | bytes 83886080 | tf_op jit(solution)/shard_map/while/body/eval_jaxpr/add | solution.py:153
  692.2 28.6 %copy.39 = bf16[512,2,1,4096]{3,1,2,0:T(2,128)(2,1)} copy(f32[512,2,1,4096]{3,0,1,2:T(8,128)} %get-tuple-element.635) | data formatting | bytes 25165824 | tf_op jit(solution)/shard_map/while | solution.py:156
  720.7 18.6 %copy.40 = bf16[512,2,1,4096]{3,1,2,0:T(2,128)(2,1)} copy(f32[512,2,1,4096]{3,0,1,2:T(8,128)S(1)} %copy-done) | data formatting | bytes 25165824 | tf_op jit(solution)/shard_map/while | solution.py:156
  (205 shorter events, 144.5 us)
Async XLA Ops:
  8.0 27.0 %copy-start.3 = (bf16[2,16,4096]{2,1,0:T(8,128)(2,1)S(1)}, bf16[2,16,4096]{2,1,0:T(8,128)(2,1)}, u32[]{:S(2)}) copy-start(bf16[2,16,4096]{2,1,0:T(8,128)(2,1)} %param.38) | copy-start | bytes 786436
  27.0 7.9 %all-to-all-start = ((bf16[4,16,1024]{2,1,0:T(8,128)(2,1)}), bf16[4,16,1024]{2,1,0:T(8,128)(2,1)S(1)}, u32[]{:S(2)}, u32[]{:S(2)}) async-start(bf16[4,16,1024]{2,1,0:T(8,128)(2,1)} %bitcast.29), calls=%async_computation | async-start | bytes 262144 | tf_op jit(solution)/shard_map/all_to_all | solution.py:71
  35.0 6.8 collective-permute-start
  61.3 6.8 collective-permute-start.1
  82.4 6.8 collective-permute-start.2
  96.5 31.5 %copy-start.4 = (bf16[2,16,4096]{2,1,0:T(8,128)(2,1)S(1)}, bf16[2,16,4096]{2,1,0:T(8,128)(2,1)}, u32[]{:S(2)}) copy-start(bf16[2,16,4096]{2,1,0:T(8,128)(2,1)} %param.41) | copy-start | bytes 786436
  103.7 7.9 %collective-permute-start.3 = (bf16[16,4096]{1,0:T(8,128)(2,1)S(1)}, bf16[16,4096]{1,0:T(8,128)(2,1)S(1)}, u32[]{:S(2)}, u32[]{:S(2)}) collective-permute-start(bf16[16,4096]{1,0:T(8,128)(2,1)S(1)} %fusion.138), channel_id=1, source_target_pairs={{0,8},{8,16},{16,24},{24,0},{1,9},{9,17},{17,25},{25,1},{2,10},{10... | collective-permute-start | bytes 393224 | tf_op jit(solution)/shard_map/ppermute | solution.py:11
  124.6 7.9 %all-to-all-start.4 = ((bf16[4,16,1024]{2,1,0:T(8,128)(2,1)}), bf16[4,16,1024]{2,1,0:T(8,128)(2,1)S(1)}, u32[]{:S(2)}, u32[]{:S(2)}) async-start(bf16[4,16,1024]{2,1,0:T(8,128)(2,1)} %bitcast.45), calls=%async_computation.4 | async-start | bytes 262144 | tf_op jit(solution)/shard_map/all_to_all | solution.py:71
  127.9 88.2 %reduce-scatter.9.cloned.1.call-start = ((), (), s32[]{:S(2)}) async-start(), calls=%async_computation.17 | async-start | bytes 655360 | tf_op jit(solution)/shard_map/reduce_scatter | solution.py:107
  132.6 8.4 %collective-permute-start.4 = (bf16[16,4096]{1,0:T(8,128)(2,1)S(1)}, bf16[16,4096]{1,0:T(8,128)(2,1)S(1)}, u32[]{:S(2)}, u32[]{:S(2)}) collective-permute-start(bf16[16,4096]{1,0:T(8,128)(2,1)S(1)} %fusion.142), channel_id=1, source_target_pairs={{0,8},{8,16},{16,24},{24,0},{1,9},{9,17},{17,25},{25,1},{2,10},{10... | collective-permute-start | bytes 393224 | tf_op jit(solution)/shard_map/ppermute | solution.py:11
  139.8 0.8 copy-start.1
  154.8 7.9 %all-to-all-start.5 = ((bf16[4,16,1024]{2,1,0:T(8,128)(2,1)}), bf16[4,16,1024]{2,1,0:T(8,128)(2,1)S(1)}, u32[]{:S(2)}, u32[]{:S(2)}) async-start(bf16[4,16,1024]{2,1,0:T(8,128)(2,1)} %bitcast.49), calls=%async_computation.5 | async-start | bytes 262144 | tf_op jit(solution)/shard_map/all_to_all | solution.py:71
  162.8 7.9 %collective-permute-start.5 = (bf16[16,4096]{1,0:T(8,128)(2,1)S(1)}, bf16[16,4096]{1,0:T(8,128)(2,1)S(1)}, u32[]{:S(2)}, u32[]{:S(2)}) collective-permute-start(bf16[16,4096]{1,0:T(8,128)(2,1)S(1)} %fusion.146), channel_id=1, source_target_pairs={{0,8},{8,16},{16,24},{24,0},{1,9},{9,17},{17,25},{25,1},{2,10},{10... | collective-permute-start | bytes 393224 | tf_op jit(solution)/shard_map/ppermute | solution.py:11
  178.6 7.9 %all-to-all-start.6 = ((bf16[4,16,1024]{2,1,0:T(8,128)(2,1)}), bf16[4,16,1024]{2,1,0:T(8,128)(2,1)S(1)}, u32[]{:S(2)}, u32[]{:S(2)}) async-start(bf16[4,16,1024]{2,1,0:T(8,128)(2,1)} %bitcast.53), calls=%async_computation.6 | async-start | bytes 262144 | tf_op jit(solution)/shard_map/all_to_all | solution.py:71
  186.6 6.8 collective-permute-start.6
  201.3 7.9 %all-to-all-start.7 = ((bf16[4,16,1024]{2,1,0:T(8,128)(2,1)}), bf16[4,16,1024]{2,1,0:T(8,128)(2,1)S(1)}, u32[]{:S(2)}, u32[]{:S(2)}) async-start(bf16[4,16,1024]{2,1,0:T(8,128)(2,1)} %bitcast.57), calls=%async_computation.7 | async-start | bytes 262144 | tf_op jit(solution)/shard_map/all_to_all | solution.py:71
  204.7 60.7 %reduce-scatter.11.cloned.1.call-start = ((), (), s32[]{:S(2)}) async-start(), calls=%async_computation.18 | async-start | bytes 655360 | tf_op jit(solution)/shard_map/reduce_scatter | solution.py:107
  209.3 6.8 collective-permute-start.7
  219.2 8.8 %collective-permute-start.8 = (bf16[16,4096]{1,0:T(8,128)(2,1)S(1)}, bf16[16,4096]{1,0:T(8,128)(2,1)S(1)}, u32[]{:S(2)}, u32[]{:S(2)}) collective-permute-start(bf16[16,4096]{1,0:T(8,128)(2,1)S(1)} %fusion.162), channel_id=1, source_target_pairs={{0,24},{8,0},{16,8},{24,16},{1,25},{9,1},{17,9},{25,17},{2,26},{10... | collective-permute-start | bytes 393224 | tf_op jit(solution)/shard_map/ppermute | solution.py:11
  235.0 0.8 copy-start.2
  235.9 73.4 %reduce-scatter.13.cloned.1.call-start = ((), (), s32[]{:S(2)}) async-start(), calls=%async_computation.19 | async-start | bytes 655360 | tf_op jit(solution)/shard_map/reduce_scatter | solution.py:107
  268.1 6.3 collective-permute-start.9
  282.6 68.5 %reduce-scatter.15.cloned.1.call-start = ((), (), s32[]{:S(2)}) async-start(), calls=%async_computation.20 | async-start | bytes 655360 | tf_op jit(solution)/shard_map/reduce_scatter | solution.py:107
  311.4 6.0 collective-permute-start.10
  331.2 65.1 %reduce-scatter.17.cloned.1.call-start = ((), (), s32[]{:S(2)}) async-start(), calls=%async_computation.21 | async-start | bytes 655360 | tf_op jit(solution)/shard_map/reduce_scatter | solution.py:107
  353.1 6.0 collective-permute-start.11
  373.0 68.7 %reduce-scatter.19.cloned.1.call-start = ((), (), s32[]{:S(2)}) async-start(), calls=%async_computation.22 | async-start | bytes 655360 | tf_op jit(solution)/shard_map/reduce_scatter | solution.py:107
  398.5 6.0 collective-permute-start.12
  412.3 73.0 %reduce-scatter.21.cloned.1.call-start = ((), (), s32[]{:S(2)}) async-start(), calls=%async_computation.23 | async-start | bytes 655360 | tf_op jit(solution)/shard_map/reduce_scatter | solution.py:107
  443.9 6.0 collective-permute-start.13
  449.9 0.6 copy-start.5
  458.5 71.8 %reduce-scatter.23.cloned.1.call-start = ((), (), s32[]{:S(2)}) async-start(), calls=%async_computation.24 | async-start | bytes 655360 | tf_op jit(solution)/shard_map/reduce_scatter | solution.py:107
  487.5 10.3 %collective-permute-start.14 = (bf16[16,4096]{1,0:T(8,128)(2,1)S(1)}, bf16[16,4096]{1,0:T(8,128)(2,1)S(1)}, u32[]{:S(2)}, u32[]{:S(2)}) collective-permute-start(bf16[16,4096]{1,0:T(8,128)(2,1)S(1)} %fusion.192), channel_id=1, source_target_pairs={{0,24},{8,0},{16,8},{24,16},{1,25},{9,1},{17,9},{25,17},{2,26},{10... | collective-permute-start | bytes 393224 | tf_op jit(solution)/shard_map/ppermute | solution.py:11
  506.4 65.1 %all-gather.4.cloned.1.call-start = ((), (), s32[]{:S(2)}) async-start(), calls=%async_computation.16 | async-start | bytes 6291456 | tf_op jit(solution)/shard_map/all_gather | solution.py:132
  512.7 117.4 %all-gather.6.cloned.1.call-start = ((), (), s32[]{:S(2)}) async-start(), calls=%async_computation.25 | async-start | bytes 6291456 | tf_op jit(solution)/shard_map/all_gather | solution.py:133
  532.4 6.0 collective-permute-start.15
  692.2 28.6 %copy-start = (f32[512,2,1,4096]{3,0,1,2:T(8,128)S(1)}, f32[512,2,1,4096]{3,0,1,2:T(8,128)}, u32[]{:S(2)}) copy-start(f32[512,2,1,4096]{3,0,1,2:T(8,128)} %get-tuple-element.634) | copy-start | bytes 50331652
Sparse Core Ops, SparseCore 0:
  140.8 28.8 reduce-scatter.8
  236.0 29.3 reduce-scatter.10
  282.7 26.5 reduce-scatter.12
  331.4 19.5 reduce-scatter.14
  373.1 23.2 reduce-scatter.16
  412.4 29.3 reduce-scatter.18
  458.6 26.6 reduce-scatter.20
  506.5 23.7 reduce-scatter.22
Sparse Core Ops, SparseCore 1:
  512.7 58.7 all-gather.3
  573.5 56.6 all-gather.5
